TPU v7x, 32 devices: a whole 2x2x4 slice. The times are simulated.
32 devices in a mesh: fsdp: 4 (over y, core), ctx: 2 (over x), tp: 4 (over z).
Axes of the slice: x: 2, y: 2, z: 4, core: 2. Of those that a mesh axis runs over, the one named last changes fastest.
Arguments:
- inputs: bfloat16 [2, 8, 512, 1024], P(None, 'fsdp', 'ctx'), may hold values from -6 to 6
- out_grad: bfloat16 [2, 8, 512, 1024], P(None, 'fsdp', 'ctx'), may hold values from -6 to 6
- segment_ids: int32 [2, 8, 512], P(None, 'fsdp'), may hold values from 0 to 7, never falling along the last dimension, each value on 1 to 256 neighbouring positions
- w_qkv: bfloat16 [1024, 3072], P(('fsdp', 'ctx'), 'tp'), may hold values from -0.25 to 0.25
- bias_qv: bfloat16 [2048], P('tp'), may hold values from -3 to 3
- w_out: bfloat16 [1024, 1024], P(('fsdp', 'ctx'), 'tp'), may hold values from -0.25 to 0.25
- w_up: bfloat16 [1024, 4096], P(('fsdp', 'ctx'), 'tp'), may hold values from -0.1875 to 0.1875
- bias_up: bfloat16 [4096], P('tp'), may hold values from -2 to 2
- w_down: bfloat16 [1024, 4096], P(('fsdp', 'ctx'), 'tp'), may hold values from -0.125 to 0.125
- gains: bfloat16 [1024, 2], P(('fsdp', 'ctx')), may hold values from 0.25 to 1.75
- shifts: bfloat16 [1024, 4], P(('fsdp', 'ctx')), may hold values from -2 to 2
Outputs:
- layer_out: bfloat16 [2, 8, 512, 1024], P(None, 'fsdp', ('ctx', 'tp'))
- input_grad: float32 [2, 8, 512, 1024], P(None, 'fsdp', ('ctx', 'tp'))
- grad_w_qkv: float32 [1024, 3072], P(('fsdp', 'ctx'), 'tp')
- grad_bias_qv: float32 [2048], P('tp')
- grad_w_out: float32 [1024, 1024], P(('fsdp', 'ctx'), 'tp')
- grad_w_up: float32 [1024, 4096], P(('fsdp', 'ctx'), 'tp')
- grad_bias_up: float32 [4096], P('tp')
- grad_w_down: float32 [1024, 4096], P(('fsdp', 'ctx'), 'tp')
- grad_gains: float32 [1024, 2], P(('fsdp', 'ctx'))
- grad_shifts: float32 [1024, 4], P(('fsdp', 'ctx'))
Inputs may be any that keep to these rules, and one draw needn't show every extreme that they name: `segment_ids`: within a sequence the ids never fall; each of the 8 documents holds 1 to 256 positions, and one holds exactly 256.
All inputs are finite; a program needn't handle non-finite values.
Results may differ from a plain program's by a relative error of at most 0.018.
Values may be sent and summed in bfloat16 or wider, within the bound.
A program may use at most 64 MiB of HBM per device.

v0:
```python
import jax
import jax.numpy as jnp
from jax import lax
from jax.sharding import PartitionSpec as P

HD = 64
norm_epsilon = 1e-12
masked_score = -1e30


def norm_rows(rows_in, gain_row, offset):
    average = jnp.mean(rows_in, axis=-1, keepdims=True)
    centered = rows_in - average
    spread = jnp.mean(centered * centered, axis=-1, keepdims=True)
    return centered * lax.rsqrt(spread + norm_epsilon) * gain_row + offset


def exact_gelu(rows_in):
    return jax.nn.gelu(rows_in, approximate=False)


def contract_rows(left_rows, right_rows):
    return lax.dot_general(
        left_rows, right_rows, (((0,), (0,)), ((), ())), preferred_element_type=jnp.float32
    )


def times_transposed(left_rows, right_rows):
    return lax.dot_general(
        left_rows, right_rows, (((1,), (1,)), ((), ())), preferred_element_type=jnp.float32
    )


def masked_scores(queries, key_rows, same_segment, score_scale):
    scores = (
        jnp.einsum("sqhe,skhe->shqk", queries, key_rows, preferred_element_type=jnp.float32)
        * score_scale
    )
    return jnp.where(same_segment[:, None], scores, masked_score)


def add_pair(running, update):
    return running + update


def reduce_rows(part):
    return lax.psum(part, "tp")


def local(
    inputs, out_grad, segment_ids, w_qkv, bias_qv, w_out, w_up, bias_up, w_down, gains, shifts
):
    batches, seq_local, rows_local, model_width = inputs.shape
    tokens = seq_local * rows_local
    heads_local = w_out.shape[1] // HD
    score_scale = HD ** (-0.5)
    row_share = rows_local // lax.axis_size("tp")
    row_start = lax.axis_index("tp") * row_share
    query_start = lax.axis_index("ctx") * rows_local
    qv_bias = bias_qv.astype(jnp.float32).reshape(heads_local, 2, HD)
    up_bias = bias_up.astype(jnp.float32)

    def pick_rows(values):
        shaped = values.reshape(seq_local, rows_local, model_width)
        return lax.dynamic_slice_in_dim(shaped, row_start, row_share, 1)

    full_totals = (
        jnp.zeros((model_width, w_qkv.shape[1]), jnp.float32),
        jnp.zeros((model_width, w_out.shape[1]), jnp.float32),
        jnp.zeros((model_width, w_up.shape[1]), jnp.float32),
        jnp.zeros((model_width, w_down.shape[1]), jnp.float32),
        jnp.zeros((model_width, 2), jnp.float32),
        jnp.zeros((model_width, 4), jnp.float32),
    )
    share_totals = (
        jnp.zeros(w_qkv.shape, jnp.float32),
        jnp.zeros(w_out.shape, jnp.float32),
        jnp.zeros(w_up.shape, jnp.float32),
        jnp.zeros(w_down.shape, jnp.float32),
        jnp.zeros(gains.shape, jnp.float32),
        jnp.zeros(shifts.shape, jnp.float32),
    )
    qv_bias_grad = jnp.zeros(bias_qv.shape, jnp.float32)
    up_bias_grad = jnp.zeros(bias_up.shape, jnp.float32)
    layer_rows = []
    input_rows = []
    for batch_index in range(batches):
        gathered = (
            lax.all_gather(w_qkv, ("fsdp", "ctx"), axis=0, tiled=True),
            lax.all_gather(w_out, ("fsdp", "ctx"), axis=0, tiled=True),
            lax.all_gather(w_up, ("fsdp", "ctx"), axis=0, tiled=True),
            lax.all_gather(w_down, ("fsdp", "ctx"), axis=0, tiled=True),
            lax.all_gather(gains, ("fsdp", "ctx"), axis=0, tiled=True),
            lax.all_gather(shifts, ("fsdp", "ctx"), axis=0, tiled=True),
        )
        full_qkv, full_out, full_up, full_down, full_gains, full_shifts = gathered
        gain_rows = full_gains.astype(jnp.float32)
        shift_rows = full_shifts.astype(jnp.float32)
        x_low = inputs[batch_index].reshape(tokens, model_width)
        x_full = x_low.astype(jnp.float32)
        projected = jnp.dot(x_low, full_qkv, preferred_element_type=jnp.float32)
        projected = projected.reshape(seq_local, rows_local, heads_local, 3, HD)
        queries = (projected[:, :, :, 0] + qv_bias[:, 0]).astype(jnp.bfloat16)
        key_local = projected[:, :, :, 1].astype(jnp.bfloat16)
        value_local = (projected[:, :, :, 2] + qv_bias[:, 1]).astype(jnp.bfloat16)
        joined = jnp.concatenate([key_local, value_local], axis=-1)
        joined_all = lax.all_gather(joined, "ctx", axis=1, tiled=True)
        key_rows = joined_all[..., :HD]
        value_rows = joined_all[..., HD:]
        segments = segment_ids[batch_index]
        query_segments = lax.dynamic_slice_in_dim(segments, query_start, rows_local, 1)
        same_segment = query_segments[:, :, None] == segments[:, None, :]
        scores = masked_scores(queries, key_rows, same_segment, score_scale)
        row_max = jnp.max(scores, axis=-1, keepdims=True)
        weights = jnp.exp(scores - row_max)
        row_total = jnp.sum(weights, axis=-1, keepdims=True)
        log_total = row_max + jnp.log(row_total)
        p_low = (weights / row_total).astype(jnp.bfloat16)
        attended = jnp.einsum(
            "shqk,skhe->sqhe", p_low, value_rows, preferred_element_type=jnp.float32
        )
        attended_low = attended.reshape(tokens, heads_local * HD).astype(jnp.bfloat16)
        attention_part = times_transposed(attended_low, full_out)
        upstream_full = out_grad[batch_index].reshape(tokens, model_width).astype(jnp.float32)
        attention_total = reduce_rows(attention_part)
        first_sum = x_full + attention_total + shift_rows[:, 0]
        first_norm, first_back = jax.vjp(norm_rows, first_sum, gain_rows[:, 0], shift_rows[:, 1])
        norm_low = first_norm.astype(jnp.bfloat16)
        before_act = jnp.dot(norm_low, full_up, preferred_element_type=jnp.float32) + up_bias
        activated, gelu_back = jax.vjp(exact_gelu, before_act)
        hidden = activated.astype(jnp.bfloat16)
        down_part = times_transposed(hidden, full_down)
        down_total = reduce_rows(down_part)
        second_sum = first_norm + down_total + shift_rows[:, 2]
        result, second_back = jax.vjp(norm_rows, second_sum, gain_rows[:, 1], shift_rows[:, 3])
        layer_rows.append(pick_rows(result).astype(jnp.bfloat16))
        second_grad, gain_two, shift_three = second_back(upstream_full)
        shift_two = jnp.sum(second_grad, axis=0)
        second_low = second_grad.astype(jnp.bfloat16)
        down_step = contract_rows(second_low, hidden)
        hidden_grad = jnp.dot(second_low, full_down, preferred_element_type=jnp.float32)
        (act_grad,) = gelu_back(hidden_grad)
        up_bias_grad = up_bias_grad + jnp.sum(act_grad, axis=0)
        act_low = act_grad.astype(jnp.bfloat16)
        up_step = contract_rows(norm_low, act_low)
        back_part = times_transposed(act_low, full_up)
        back_total = reduce_rows(back_part)
        norm_grad = second_grad + back_total
        first_grad, gain_one, shift_one = first_back(norm_grad)
        shift_zero = jnp.sum(first_grad, axis=0)
        first_low = first_grad.astype(jnp.bfloat16)
        out_step = contract_rows(first_low, attended_low)
        attended_grad = jnp.dot(first_low, full_out, preferred_element_type=jnp.float32)
        attended_grad = attended_grad.astype(jnp.bfloat16).reshape(
            seq_local, rows_local, heads_local, HD
        )
        scores = masked_scores(queries, key_rows, same_segment, score_scale)
        probabilities = jnp.exp(scores - log_total)
        value_grad = jnp.einsum(
            "shqk,sqhe->skhe",
            probabilities.astype(jnp.bfloat16),
            attended_grad,
            preferred_element_type=jnp.float32,
        )
        prob_grad = jnp.einsum(
            "sqhe,skhe->shqk", attended_grad, value_rows, preferred_element_type=jnp.float32
        )
        row_dot = jnp.sum(prob_grad * probabilities, axis=-1, keepdims=True)
        score_grad = (probabilities * (prob_grad - row_dot)).astype(jnp.bfloat16)
        query_grad = (
            jnp.einsum("shqk,skhe->sqhe", score_grad, key_rows, preferred_element_type=jnp.float32)
            * score_scale
        )
        key_grad = (
            jnp.einsum("shqk,sqhe->skhe", score_grad, queries, preferred_element_type=jnp.float32)
            * score_scale
        )
        kv_grads = lax.psum_scatter(
            jnp.concatenate([key_grad, value_grad], axis=-1).astype(jnp.bfloat16),
            "ctx",
            scatter_dimension=1,
            tiled=True,
        ).astype(jnp.float32)
        key_mine = kv_grads[..., :HD]
        value_mine = kv_grads[..., HD:]
        bias_step = jnp.stack(
            [jnp.sum(query_grad, axis=(0, 1)), jnp.sum(value_mine, axis=(0, 1))], axis=1
        )
        qv_bias_grad = qv_bias_grad + bias_step.reshape(-1)
        mixed_grad = jnp.stack([query_grad, key_mine, value_mine], axis=3)
        mixed_grad = mixed_grad.reshape(tokens, 3 * heads_local * HD).astype(jnp.bfloat16)
        qkv_step = contract_rows(x_low, mixed_grad)
        input_part = times_transposed(mixed_grad, full_qkv).reshape(
            seq_local, rows_local, model_width
        )
        input_mine = lax.psum_scatter(
            input_part.astype(jnp.bfloat16), "tp", scatter_dimension=1, tiled=True
        ).astype(jnp.float32)
        first_part = pick_rows(first_grad)
        input_rows.append(input_mine + first_part)
        gain_step = jnp.stack([gain_one, gain_two], axis=1)
        shift_step = jnp.stack([shift_zero, shift_one, shift_two, shift_three], axis=1)
        full_totals = tuple(
            map(
                add_pair,
                full_totals,
                (qkv_step, out_step, up_step, down_step, gain_step, shift_step),
            )
        )
    share_totals = (
        lax.psum_scatter(
            full_totals[0].astype(jnp.bfloat16), ("fsdp", "ctx"), scatter_dimension=0, tiled=True
        ).astype(jnp.float32),
        lax.psum_scatter(
            full_totals[1].astype(jnp.bfloat16), ("fsdp", "ctx"), scatter_dimension=0, tiled=True
        ).astype(jnp.float32),
        lax.psum_scatter(
            full_totals[2].astype(jnp.bfloat16), ("fsdp", "ctx"), scatter_dimension=0, tiled=True
        ).astype(jnp.float32),
        lax.psum_scatter(
            full_totals[3].astype(jnp.bfloat16), ("fsdp", "ctx"), scatter_dimension=0, tiled=True
        ).astype(jnp.float32),
        lax.psum_scatter(
            full_totals[4].astype(jnp.bfloat16), ("fsdp", "ctx"), scatter_dimension=0, tiled=True
        ).astype(jnp.float32),
        lax.psum_scatter(
            full_totals[5].astype(jnp.bfloat16), ("fsdp", "ctx"), scatter_dimension=0, tiled=True
        ).astype(jnp.float32),
    )
    qv_total, up_total = lax.psum((qv_bias_grad, up_bias_grad), ("fsdp", "ctx"))
    return (
        jnp.stack(layer_rows, axis=0),
        jnp.stack(input_rows, axis=0),
        share_totals[0],
        qv_total,
        share_totals[1],
        share_totals[2],
        up_total,
        share_totals[3],
        share_totals[4],
        share_totals[5],
    )


def solution(mesh):
    placed = (
        P(None, "fsdp", "ctx", None),
        P(None, "fsdp", "ctx", None),
        P(None, "fsdp", None),
        P(("fsdp", "ctx"), "tp"),
        P("tp"),
        P(("fsdp", "ctx"), "tp"),
        P(("fsdp", "ctx"), "tp"),
        P("tp"),
        P(("fsdp", "ctx"), "tp"),
        P(("fsdp", "ctx"), None),
        P(("fsdp", "ctx"), None),
    )
    return jax.shard_map(
        local,
        mesh=mesh,
        in_specs=placed,
        out_specs=(
            P(None, "fsdp", ("ctx", "tp"), None),
            P(None, "fsdp", ("ctx", "tp"), None),
            P(("fsdp", "ctx"), "tp"),
            P("tp"),
            P(("fsdp", "ctx"), "tp"),
            P(("fsdp", "ctx"), "tp"),
            P("tp"),
            P(("fsdp", "ctx"), "tp"),
            P(("fsdp", "ctx"), None),
            P(("fsdp", "ctx"), None),
        ),
        check_vma=False,
    )
```

profile of v0, /device:TPU:0, one launch (start us, length us, event | category | flops | bytes accessed | tf_op | source)
XLA Modules:
  0.0 1028.2 jit_solution(4687349844855321863)
XLA Ops:
  9.5 28.8 %all-gather.6.cloned.1.call-done = bf16[1024,768]{1,0:T(8,128)(2,1)} async-done(((bf16[128,768]{1,0:T(8,128)(2,1)}), bf16[1024,768]{1,0:T(8,128)(2,1)}) %all-gather.6.cloned.1.call-update) | async-done | bytes 1572880 | tf_op jit(solution)/shard_map/all_gather | solution.py:89
  45.8 19.5 %all_gather.32 = bf16[1024,256]{1,0:T(8,128)(2,1)S(1)} all-gather(bf16[128,256]{1,0:T(8,128)(2,1)S(1)} %copy-done.39), channel_id=1, replica_groups=mesh['fsdp'=4,'ctx'=2,'tp'=4] {'fsdp','ctx'}, dimensions={0}, use_global_device_ids=true | all-gather | bytes 589824 | tf_op jit(solution)/shard_map/all_gather | solution.py:90
  75.9 17.4 %all-gather.14.cloned.1.call-done = bf16[2,512,4,128]{1,3,2,0:T(8,128)(2,1)} async-done(((bf16[2,256,4,128]{1,3,2,0:T(8,128)(2,1)}), bf16[2,512,4,128]{1,3,2,0:T(8,128)(2,1)}) %all-gather.14.cloned.1.call-update) | async-done | bytes 1048592 | tf_op jit(solution)/shard_map/all_gather | solution.py:107
  106.2 12.1 %all_gather.33 = bf16[1024,4]{0,1:T(4,128)(2,1)S(1)} all-gather(bf16[128,4]{0,1:T(4,128)(2,1)S(1)} %copy-done.41), channel_id=1, replica_groups=mesh['fsdp'=4,'ctx'=2,'tp'=4] {'fsdp','ctx'}, dimensions={0}, use_global_device_ids=true | all-gather | bytes 9216 | tf_op jit(solution)/shard_map/all_gather | solution.py:94
  118.4 10.9 %all_gather.34 = bf16[1024,2]{0,1:T(2,128)(2,1)S(1)} all-gather(bf16[128,2]{0,1:T(2,128)(2,1)S(1)} %copy-done.42), channel_id=1, replica_groups=mesh['fsdp'=4,'ctx'=2,'tp'=4] {'fsdp','ctx'}, dimensions={0}, use_global_device_ids=true | all-gather | bytes 4608 | tf_op jit(solution)/shard_map/all_gather | solution.py:93
  129.3 129.0 %all-reduce.12.cloned.1.call-done = (f32[512,1024]{1,0:T(8,128)}, f32[512,1024]{1,0:T(8,128)}) async-done(((f32[512,1024]{1,0:T(8,128)}, f32[512,1024]{1,0:T(8,128)}), (f32[512,1024]{1,0:T(8,128)}, f32[512,1024]{1,0:T(8,128)})) %all-reduce.12.cloned.1.call-update) | async-done | bytes 4194320 | tf_op jit(solution)/shard_map/psum | solution.py:47
  258.3 3.4 fusion.135
  263.1 23.7 %all-gather.10.cloned.1.call-done = bf16[1024,1024]{1,0:T(8,128)(2,1)} async-done(((bf16[128,1024]{1,0:T(8,128)(2,1)}), bf16[1024,1024]{1,0:T(8,128)(2,1)}) %all-gather.10.cloned.1.call-update) | async-done | bytes 2097168 | tf_op jit(solution)/shard_map/all_gather | solution.py:91
  286.8 3.7 fusion.124
  291.9 11.7 %multiply_convert_fusion.2 = (bf16[512,1024]{1,0:T(8,128)(2,1)}, f32[512,1024]{1,0:T(8,128)}, bf16[512,1024]{1,0:T(8,128)(2,1)}, f32[512,1024]{1,0:T(8,128)}, f32[512,1024]{1,0:T(8,128)}) fusion(f32[1024]{0:T(1024)S(1)} %convert_element_type.236, f32[512,1024]{1,0:T(8,128)S(1)} %fusion.124, bf16[1024,1024]{1,0:T(8,128)(2,1)S(1)} %copy-done.43, ...), kind=kOutput, calls=%fused_computation.54 | convolution fusion | flops 1145569280 | bytes 14696448 | tf_op jit(solution)/shard_map/dot_general | solution.py:129
  303.6 12.8 %all-gather.12.cloned.1.call-done = bf16[1024,1024]{1,0:T(8,128)(2,1)} async-done(((bf16[128,1024]{1,0:T(8,128)(2,1)}), bf16[1024,1024]{1,0:T(8,128)(2,1)}) %all-gather.12.cloned.1.call-update) | async-done | bytes 2097168 | tf_op jit(solution)/shard_map/all_gather | solution.py:92
  316.4 4.7 fusion.148
  324.2 154.7 %all-reduce.10.cloned.1.call-done = (f32[512,1024]{1,0:T(8,128)}, f32[512,1024]{1,0:T(8,128)}) async-done(((f32[512,1024]{1,0:T(8,128)}, f32[512,1024]{1,0:T(8,128)}), (f32[512,1024]{1,0:T(8,128)}, f32[512,1024]{1,0:T(8,128)})) %all-reduce.10.cloned.1.call-update) | async-done | bytes 4194320 | tf_op jit(solution)/shard_map/psum | solution.py:47
  478.9 4.2 fusion.132
  501.7 153.9 %all-reduce.8.cloned.1.call-done = (f32[512,1024]{1,0:T(8,128)}, f32[512,1024]{1,0:T(8,128)}) async-done(((f32[512,1024]{1,0:T(8,128)}, f32[512,1024]{1,0:T(8,128)}), (f32[512,1024]{1,0:T(8,128)}, f32[512,1024]{1,0:T(8,128)})) %all-reduce.8.cloned.1.call-update) | async-done | bytes 4194320 | tf_op jit(solution)/shard_map/psum | solution.py:47
  655.6 4.0 multiply_reduce_fusion.2
  669.3 3.2 fusion.56
  682.9 4.0 multiply_reduce_fusion.1
  692.0 3.4 fusion.87
  695.5 2.9 add_convert_fusion.1
  698.6 3.4 fusion.115
  702.0 2.8 add_convert_fusion
  710.9 2.9 fusion.49
  742.3 24.5 %reduce-scatter.27.cloned.1.call-done = bf16[128,1024]{1,0:T(8,128)(2,1)} async-done(((bf16[1024,1024]{1,0:T(8,128)(2,1)}), bf16[128,1024]{1,0:T(8,128)(2,1)}) %reduce-scatter.27.cloned.1.call-update) | async-done | bytes 262160 | tf_op jit(solution)/shard_map/reduce_scatter | solution.py:217
  768.5 42.5 %reduce-scatter.29.cloned.1.call-done = bf16[128,1024]{1,0:T(8,128)(2,1)} async-done(((bf16[1024,1024]{1,0:T(8,128)(2,1)}), bf16[128,1024]{1,0:T(8,128)(2,1)}) %reduce-scatter.29.cloned.1.call-update) | async-done | bytes 262160 | tf_op jit(solution)/shard_map/reduce_scatter | solution.py:220
  812.8 35.0 %reduce-scatter.33.cloned.1.call-done = bf16[128,2]{1,0:T(8,128)(2,1)} async-done(((bf16[1024,2]{1,0:T(8,128)(2,1)}), bf16[128,2]{1,0:T(8,128)(2,1)}) %reduce-scatter.33.cloned.1.call-update) | async-done | bytes 528
  849.2 35.2 %reduce-scatter.35.cloned.1.call-done = bf16[128,4]{1,0:T(8,128)(2,1)} async-done(((bf16[1024,4]{1,0:T(8,128)(2,1)}), bf16[128,4]{1,0:T(8,128)(2,1)}) %reduce-scatter.35.cloned.1.call-update) | async-done | bytes 1040
  885.8 35.7 %reduce-scatter.25.cloned.1.call-done = bf16[128,256]{1,0:T(8,128)(2,1)} async-done(((bf16[1024,256]{1,0:T(8,128)(2,1)}), bf16[128,256]{1,0:T(8,128)(2,1)}) %reduce-scatter.25.cloned.1.call-update) | async-done | bytes 65552 | tf_op jit(solution)/shard_map/reduce_scatter | solution.py:214
  923.3 14.3 %all-reduce = (f32[512]{0:T(512)}, f32[1024]{0:T(1024)}) all-reduce(f32[512]{0:T(512)S(1)} %add.309, f32[1024]{0:T(1024)S(1)} %add.312), channel_id=1, replica_groups=mesh['fsdp'=4,'ctx'=2,'tp'=4] {'fsdp','ctx'}, use_global_device_ids=true, to_apply=%region_37.38 | all-reduce | flops 1536 | bytes 12288 | tf_op jit(solution)/shard_map/psum | solution.py:230
  937.6 13.3 %reduce-scatter.23.cloned.1.call-done = bf16[2,64,1024]{2,1,0:T(8,128)(2,1)} async-done(((bf16[2,256,1024]{2,1,0:T(8,128)(2,1)}), bf16[2,64,1024]{2,1,0:T(8,128)(2,1)}) %reduce-scatter.23.cloned.1.call-update) | async-done | bytes 262160 | tf_op jit(solution)/shard_map/reduce_scatter | solution.py:196
  952.1 26.8 %reduce-scatter.19.cloned.1.call-done = bf16[2,64,1024]{2,1,0:T(8,128)(2,1)} async-done(((bf16[2,256,1024]{2,1,0:T(8,128)(2,1)}), bf16[2,64,1024]{2,1,0:T(8,128)(2,1)}) %reduce-scatter.19.cloned.1.call-update) | async-done | bytes 262160 | tf_op jit(solution)/shard_map/reduce_scatter | solution.py:196
  981.1 37.8 %reduce-scatter.31.cloned.1.call-done = bf16[128,768]{1,0:T(8,128)(2,1)} async-done(((bf16[1024,768]{1,0:T(8,128)(2,1)}), bf16[128,768]{1,0:T(8,128)(2,1)}) %reduce-scatter.31.cloned.1.call-update) | async-done | bytes 196624
  (271 shorter events, 130.2 us)
Async XLA Ops:
  7.2 33.6 %copy-start.31 = (bf16[2,2,256,1024]{3,2,1,0:T(8,128)(2,1)S(1)}, bf16[2,2,256,1024]{3,2,1,0:T(8,128)(2,1)}, u32[]{:S(2)}) copy-start(bf16[2,2,256,1024]{3,2,1,0:T(8,128)(2,1)} %param.11) | copy-start | bytes 6291460
  7.2 31.0 %all-gather.6.cloned.1.call-start = ((), (), s32[]{:S(2)}) async-start(), calls=%async_computation.10 | async-start | bytes 1769472 | tf_op jit(solution)/shard_map/all_gather | solution.py:89
  7.9 62.1 %all-gather.8.cloned.1.call-start = ((), (), s32[]{:S(2)}) async-start(), calls=%async_computation.11 | async-start | bytes 1572864 | tf_op jit(solution)/shard_map/all_gather | solution.py:107
  44.4 25.5 %copy-start.28 = (f32[2,256,4,3,64]{1,4,3,2,0:T(8,128)}, f32[2,256,4,3,64]{1,4,3,2,0:T(8,128)S(1)}, u32[]{:S(2)}) copy-start(f32[2,256,4,3,64]{1,4,3,2,0:T(8,128)S(1)} %fusion.69) | copy-start | bytes 4718596
  45.8 47.6 %all-gather.14.cloned.1.call-start = ((), (), s32[]{:S(2)}) async-start(), calls=%async_computation.14 | async-start | bytes 1572864 | tf_op jit(solution)/shard_map/all_gather | solution.py:107
  67.7 190.6 %all-reduce.12.cloned.1.call-start = ((), (), s32[]{:S(2)}) async-start(), calls=%async_computation.27 | async-start | bytes 8388608 | tf_op jit(solution)/shard_map/psum | solution.py:47
  103.1 183.7 %all-gather.10.cloned.1.call-start = ((), (), s32[]{:S(2)}) async-start(), calls=%async_computation.12 | async-start | bytes 2359296 | tf_op jit(solution)/shard_map/all_gather | solution.py:91
  103.7 212.7 %all-gather.12.cloned.1.call-start = ((), (), s32[]{:S(2)}) async-start(), calls=%async_computation.13 | async-start | bytes 2359296 | tf_op jit(solution)/shard_map/all_gather | solution.py:92
  104.3 14.0 %copy-start.40 = (bf16[1024]{0:T(1024)(128)(2,1)S(1)}, bf16[1024]{0:T(1024)(128)(2,1)}, u32[]{:S(2)}) copy-start(bf16[1024]{0:T(1024)(128)(2,1)} %param.18) | copy-start | bytes 6148
  104.3 14.0 %copy-start.42 = (bf16[128,2]{0,1:T(2,128)(2,1)S(1)}, bf16[128,2]{0,1:T(2,128)(2,1)}, u32[]{:S(2)}) copy-start(bf16[128,2]{0,1:T(2,128)(2,1)} %param.20) | copy-start | bytes 1540
  104.3 374.5 %all-reduce.10.cloned.1.call-start = ((), (), s32[]{:S(2)}) async-start(), calls=%async_computation.26 | async-start | bytes 8388608 | tf_op jit(solution)/shard_map/psum | solution.py:47
  261.7 28.8 %copy-start.5 = (f32[512,1024]{1,0:T(8,128)}, f32[512,1024]{1,0:T(8,128)S(1)}, u32[]{:S(2)}) copy-start(f32[512,1024]{1,0:T(8,128)S(1)} %get-tuple-element.83) | copy-start | bytes 6291460
  286.8 5.0 copy-start.43
  316.4 4.7 copy-start.37
  316.4 4.7 copy-start.45
  323.7 331.9 %all-reduce.8.cloned.1.call-start = ((), (), s32[]{:S(2)}) async-start(), calls=%async_computation.25 | async-start | bytes 8388608 | tf_op jit(solution)/shard_map/psum | solution.py:47
  483.1 4.2 copy-start.4
  489.0 6.1 copy-start.13
  501.4 215.0 %reduce-scatter.21.cloned.1.call-start = ((), (), s32[]{:S(2)}) async-start(), calls=%async_computation.17 | async-start | bytes 1572864 | tf_op jit(solution)/shard_map/reduce_scatter | solution.py:178
  655.6 4.7 copy-start.11
  655.6 5.3 copy-start.30
  680.3 44.0 %reduce-scatter.17.cloned.1.call-start = ((), (), s32[]{:S(2)}) async-start(), calls=%async_computation.15 | async-start | bytes 1572864 | tf_op jit(solution)/shard_map/reduce_scatter | solution.py:178
  691.8 75.0 %reduce-scatter.27.cloned.1.call-start = ((), (), s32[]{:S(2)}) async-start(), calls=%async_computation.20 | async-start | bytes 2359296 | tf_op jit(solution)/shard_map/reduce_scatter | solution.py:217
  698.5 112.5 %reduce-scatter.29.cloned.1.call-start = ((), (), s32[]{:S(2)}) async-start(), calls=%async_computation.21 | async-start | bytes 2359296 | tf_op jit(solution)/shard_map/reduce_scatter | solution.py:220
  704.9 142.9 %reduce-scatter.33.cloned.1.call-start = ((), (), s32[]{:S(2)}) async-start(), calls=%async_computation.23 | async-start | bytes 294912
  709.8 174.5 %reduce-scatter.35.cloned.1.call-start = ((), (), s32[]{:S(2)}) async-start(), calls=%async_computation.24 | async-start | bytes 294912
  710.8 210.6 %reduce-scatter.25.cloned.1.call-start = ((), (), s32[]{:S(2)}) async-start(), calls=%async_computation.19 | async-start | bytes 589824 | tf_op jit(solution)/shard_map/reduce_scatter | solution.py:214
  713.8 237.1 %reduce-scatter.23.cloned.1.call-start = ((), (), s32[]{:S(2)}) async-start(), calls=%async_computation.18 | async-start | bytes 1310720 | tf_op jit(solution)/shard_map/reduce_scatter | solution.py:196
  721.5 257.3 %reduce-scatter.19.cloned.1.call-start = ((), (), s32[]{:S(2)}) async-start(), calls=%async_computation.16 | async-start | bytes 1310720 | tf_op jit(solution)/shard_map/reduce_scatter | solution.py:196
  729.4 289.4 %reduce-scatter.31.cloned.1.call-start = ((), (), s32[]{:S(2)}) async-start(), calls=%async_computation.22 | async-start | bytes 1769472
  741.4 181.6 %copy-start.24 = (f32[2,256,4,128]{1,3,2,0:T(8,128)S(1)}, f32[2,256,4,128]{1,3,2,0:T(8,128)}, u32[]{:S(2)}) copy-start(f32[2,256,4,128]{1,3,2,0:T(8,128)} %copy-done.23) | copy-start | bytes 3145732
  741.4 181.7 %copy-start.22 = (f32[2,256,4,128]{1,3,2,0:T(8,128)S(1)}, f32[2,256,4,128]{1,3,2,0:T(8,128)}, u32[]{:S(2)}) copy-start(f32[2,256,4,128]{1,3,2,0:T(8,128)} %copy-done.21) | copy-start | bytes 3145732
  (41 other events, 94.5 us)
Sparse Core Ops, SparseCore 0:
  9.9 28.2 all-gather.5
  45.9 24.0 all-gather.7
  72.1 21.2 all-gather.13
  103.3 155.0 all-reduce.11
  260.1 26.7 all-gather.9
  288.6 27.7 all-gather.11
  323.8 155.0 all-reduce.9
  501.6 153.9 all-reduce.7
  680.4 19.3 reduce-scatter.20
  701.9 20.3 reduce-scatter.16
  725.6 41.1 reduce-scatter.26
  769.9 41.0 reduce-scatter.28
  814.0 33.6 reduce-scatter.32
  850.6 33.6 reduce-scatter.34
  887.3 34.1 reduce-scatter.24
  923.6 27.2 reduce-scatter.22
  953.0 25.7 reduce-scatter.18
  982.0 36.8 reduce-scatter.30
where the time goes:
time: 1040 us; the launch traced here: 1030 us
  waiting for transfers between devices  775 us (75%)
  matrix products  93.1 us (9%)
  blocking collectives  56.8 us (5%)
  other arithmetic  47.2 us (5%)
  local copies, waits for them, and re-layouts  38.3 us (4%)
  between operations  15.8 us (2%)
    psum x3, waiting for transfers between devices, reduce_rows(): return lax.psum(part, 'tp')  438 us
    unnamed x21, waiting for transfers between devices  110 us
    reduce_scatter x1, waiting for transfers between devices, local(): lax.psum_scatter(full_totals[3].astype(jnp.bfloat16), ('fsdp', 'ctx'), sc...  42.5 us
    reduce_scatter x2, waiting for transfers between devices, local(): lax.psum_scatter(input_part.astype(jnp.bfloat16), 'tp', scatter_dimension...  40.1 us
    reduce_scatter x1, waiting for transfers between devices, local(): lax.psum_scatter(full_totals[1].astype(jnp.bfloat16), ('fsdp', 'ctx'), sc...  35.7 us
    all_gather x1, waiting for transfers between devices, local(): lax.all_gather(w_qkv, ('fsdp', 'ctx'), axis=0, tiled=True)  28.8 us
    unnamed x121, local copies, waits for them, and re-layouts  25.1 us
    reduce_scatter x1, waiting for transfers between devices, local(): lax.psum_scatter(full_totals[2].astype(jnp.bfloat16), ('fsdp', 'ctx'), sc...  24.5 us
  transfers between devices with their start and end apart: 18, of which 16 were waited for; matrix products, arithmetic and copies ran while one was open for 10% of the time, Pallas kernels for 0%

commit v1 on v0

--- a/solution.py
+++ b/solution.py
@@ -2,10 +2,37 @@
 import jax.numpy as jnp
 from jax import lax
 from jax.sharding import PartitionSpec as P
+from jax.lax import axis_index, axis_size, ppermute
 
 HD = 64
 norm_epsilon = 1e-12
 masked_score = -1e30
+
+
+def paths_edit(array_in):
+    net_axis = ("fsdp", "ctx")
+    val = axis_size(net_axis)
+    part_now = axis_index(net_axis)
+    o_now, arr_now, taken_in = (val, part_now, array_in.shape[0])
+    fields = [(t, (t + 1) % o_now) for t in range(o_now)]
+    grid = [(t, (t - 1) % o_now) for t in range(o_now)]
+    frame_out = jnp.zeros(
+        (*array_in.shape[:0], o_now * taken_in, *array_in.shape[1:]), array_in.dtype
+    )
+    frame_out = lax.dynamic_update_slice_in_dim(frame_out, array_in, arr_now * taken_in, axis=0)
+    passed = all_values = array_in
+    block_last = o_now // 2
+    for ii in range(1, block_last + 1):
+        passed = ppermute(passed, net_axis, perm=fields)
+        frame_out = lax.dynamic_update_slice_in_dim(
+            frame_out, passed, (arr_now - ii) % o_now * taken_in, axis=0
+        )
+        if ii < o_now - block_last:
+            all_values = ppermute(all_values, net_axis, grid)
+            frame_out = lax.dynamic_update_slice_in_dim(
+                frame_out, all_values, (arr_now + ii) % o_now * taken_in, axis=0
+            )
+    return frame_out
 
 
 def norm_rows(rows_in, gain_row, offset):
@@ -86,7 +113,7 @@
     input_rows = []
     for batch_index in range(batches):
         gathered = (
-            lax.all_gather(w_qkv, ("fsdp", "ctx"), axis=0, tiled=True),
+            paths_edit(w_qkv),
             lax.all_gather(w_out, ("fsdp", "ctx"), axis=0, tiled=True),
             lax.all_gather(w_up, ("fsdp", "ctx"), axis=0, tiled=True),
             lax.all_gather(w_down, ("fsdp", "ctx"), axis=0, tiled=True),

time: 1040 us -> 1010 us (0.971)
  waiting for transfers between devices: 775 us -> 718 us
  starting transfers between devices: 1.78 us -> 18.3 us
    all_gather x1 -> x0, waiting for transfers between devices: 28.8 us -> none  [local(): lax.all_gather(w_qkv, ('fsdp', 'ctx'), axis=0, tiled=True)]
    all_gather x1, waiting for transfers between devices: 23.7 us -> 0.01 us  [local(): lax.all_gather(w_up, ('fsdp', 'ctx'), axis=0, tiled=True)]
    ppermute x0 -> x7, starting transfers between devices: none -> 16.3 us  [the longest x4 10.4 us: paths_edit(): passed = ppermute(passed, net_axis, perm=fields)]
    all_gather x1, waiting for transfers between devices: 12.8 us -> 0.01 us  [local(): lax.all_gather(w_down, ('fsdp', 'ctx'), axis=0, tiled=True)]
    unnamed x121 -> x131, local copies, waits for them, and re-layouts: 25.1 us -> 24.6 us
    unnamed x21 -> x20, waiting for transfers between devices: 110 us -> 110 us
  transfers between devices with their start and end apart: 18 -> 24, of which waited for: 16 -> 18; matrix products, arithmetic and copies ran while one was open for 10% -> 11% of each run, Pallas kernels for 0% -> 0%
where the time goes in v1:
time: 1010 us; the launch traced here: 1000 us
  waiting for transfers between devices  718 us (71%)
  matrix products  97 us (10%)
  blocking collectives  57.5 us (6%)
  other arithmetic  48.4 us (5%)
  local copies, waits for them, and re-layouts  48.1 us (5%)
  starting transfers between devices  18.3 us (2%)
  between operations  16.7 us (2%)
    psum x3, waiting for transfers between devices, reduce_rows(): return lax.psum(part, 'tp')  438 us
    unnamed x20, waiting for transfers between devices  110 us
    reduce_scatter x1, waiting for transfers between devices, local(): lax.psum_scatter(full_totals[3].astype(jnp.bfloat16), ('fsdp', 'ctx'), sc...  42.7 us
    reduce_scatter x2, waiting for transfers between devices, local(): lax.psum_scatter(input_part.astype(jnp.bfloat16), 'tp', scatter_dimension...  40.2 us
    reduce_scatter x1, waiting for transfers between devices, local(): lax.psum_scatter(full_totals[1].astype(jnp.bfloat16), ('fsdp', 'ctx'), sc...  35.7 us
    unnamed x131, local copies, waits for them, and re-layouts  24.6 us
    dot_general x8, matrix products, times_transposed(): lax.dot_general(left_rows, right_rows, (((1,), (1,)), ((), ())), preferre...  23.1 us
    reduce_scatter x1, waiting for transfers between devices, local(): lax.psum_scatter(full_totals[2].astype(jnp.bfloat16), ('fsdp', 'ctx'), sc...  22.2 us
  transfers between devices with their start and end apart: 24, of which 18 were waited for; matrix products, arithmetic and copies ran while one was open for 11% of the time, Pallas kernels for 0%

profile of v1, /device:TPU:0, one launch (start us, length us, event | category | flops | bytes accessed | tf_op | source)
XLA Modules:
  0.0 1004.2 jit_solution(1088559569363354977)
XLA Ops:
  8.1 3.0 collective-permute-start
  38.3 3.4 collective-permute-done.6
  42.4 3.6 convolution_bitcast_fusion.1
  49.6 3.6 convolution_bitcast_fusion
  58.3 19.9 %all_gather.27 = bf16[1024,256]{1,0:T(8,128)(2,1)S(1)} all-gather(bf16[128,256]{1,0:T(8,128)(2,1)S(1)} %copy-done.41), channel_id=1, replica_groups=mesh['fsdp'=4,'ctx'=2,'tp'=4] {'fsdp','ctx'}, dimensions={0}, use_global_device_ids=true | all-gather | bytes 589824 | tf_op jit(solution)/shard_map/all_gather | solution.py:117
  89.6 17.4 %all-gather.11.cloned.1.call-done = bf16[2,512,4,128]{1,3,2,0:T(8,128)(2,1)} async-done(((bf16[2,256,4,128]{1,3,2,0:T(8,128)(2,1)}), bf16[2,512,4,128]{1,3,2,0:T(8,128)(2,1)}) %all-gather.11.cloned.1.call-update) | async-done | bytes 1048592 | tf_op jit(solution)/shard_map/all_gather | solution.py:134
  117.9 12.3 %all_gather.28 = bf16[1024,4]{0,1:T(4,128)(2,1)S(1)} all-gather(bf16[128,4]{0,1:T(4,128)(2,1)S(1)} %copy-done.45), channel_id=1, replica_groups=mesh['fsdp'=4,'ctx'=2,'tp'=4] {'fsdp','ctx'}, dimensions={0}, use_global_device_ids=true | all-gather | bytes 9216 | tf_op jit(solution)/shard_map/all_gather | solution.py:121
  130.2 11.0 %all_gather.29 = bf16[1024,2]{0,1:T(2,128)(2,1)S(1)} all-gather(bf16[128,2]{0,1:T(2,128)(2,1)S(1)} %copy-done.46), channel_id=1, replica_groups=mesh['fsdp'=4,'ctx'=2,'tp'=4] {'fsdp','ctx'}, dimensions={0}, use_global_device_ids=true | all-gather | bytes 4608 | tf_op jit(solution)/shard_map/all_gather | solution.py:120
  141.2 130.6 %all-reduce.12.cloned.1.call-done = (f32[512,1024]{1,0:T(8,128)}, f32[512,1024]{1,0:T(8,128)}) async-done(((f32[512,1024]{1,0:T(8,128)}, f32[512,1024]{1,0:T(8,128)}), (f32[512,1024]{1,0:T(8,128)}, f32[512,1024]{1,0:T(8,128)})) %all-reduce.12.cloned.1.call-update) | async-done | bytes 4194320 | tf_op jit(solution)/shard_map/psum | solution.py:74
  271.9 3.5 fusion.130
  276.7 3.7 fusion.119
  281.8 11.7 %multiply_convert_fusion.2 = (bf16[512,1024]{1,0:T(8,128)(2,1)}, f32[512,1024]{1,0:T(8,128)}, bf16[512,1024]{1,0:T(8,128)(2,1)}, f32[512,1024]{1,0:T(8,128)}, f32[512,1024]{1,0:T(8,128)}) fusion(f32[1024]{0:T(1024)S(1)} %convert_element_type.236, f32[512,1024]{1,0:T(8,128)S(1)} %fusion.119, bf16[1024,1024]{1,0:T(8,128)(2,1)S(1)} %copy-done.47, ...), kind=kOutput, calls=%fused_computation.54 | convolution fusion | flops 1145569280 | bytes 14696448 | tf_op jit(solution)/shard_map/dot_general | solution.py:156
  293.5 4.7 fusion.145
  301.1 153.8 %all-reduce.10.cloned.1.call-done = (f32[512,1024]{1,0:T(8,128)}, f32[512,1024]{1,0:T(8,128)}) async-done(((f32[512,1024]{1,0:T(8,128)}, f32[512,1024]{1,0:T(8,128)}), (f32[512,1024]{1,0:T(8,128)}, f32[512,1024]{1,0:T(8,128)})) %all-reduce.10.cloned.1.call-update) | async-done | bytes 4194320 | tf_op jit(solution)/shard_map/psum | solution.py:74
  455.0 4.2 fusion.127
  478.1 153.6 %all-reduce.8.cloned.1.call-done = (f32[512,1024]{1,0:T(8,128)}, f32[512,1024]{1,0:T(8,128)}) async-done(((f32[512,1024]{1,0:T(8,128)}, f32[512,1024]{1,0:T(8,128)}), (f32[512,1024]{1,0:T(8,128)}, f32[512,1024]{1,0:T(8,128)})) %all-reduce.8.cloned.1.call-update) | async-done | bytes 4194320 | tf_op jit(solution)/shard_map/psum | solution.py:74
  631.7 4.0 multiply_reduce_fusion.2
  645.4 3.2 fusion.54
  659.7 4.1 multiply_reduce_fusion.1
  667.5 3.4 fusion.82
  674.0 3.4 fusion.112
  694.1 3.5 fusion.41
  703.5 3.4 fusion.38
  719.7 22.2 %reduce-scatter.27.cloned.1.call-done = bf16[128,1024]{1,0:T(8,128)(2,1)} async-done(((bf16[1024,1024]{1,0:T(8,128)(2,1)}), bf16[128,1024]{1,0:T(8,128)(2,1)}) %reduce-scatter.27.cloned.1.call-update) | async-done | bytes 262160 | tf_op jit(solution)/shard_map/reduce_scatter | solution.py:244
  743.7 42.7 %reduce-scatter.29.cloned.1.call-done = bf16[128,1024]{1,0:T(8,128)(2,1)} async-done(((bf16[1024,1024]{1,0:T(8,128)(2,1)}), bf16[128,1024]{1,0:T(8,128)(2,1)}) %reduce-scatter.29.cloned.1.call-update) | async-done | bytes 262160 | tf_op jit(solution)/shard_map/reduce_scatter | solution.py:247
  788.2 34.8 %reduce-scatter.33.cloned.1.call-done = bf16[128,2]{1,0:T(8,128)(2,1)} async-done(((bf16[1024,2]{1,0:T(8,128)(2,1)}), bf16[128,2]{1,0:T(8,128)(2,1)}) %reduce-scatter.33.cloned.1.call-update) | async-done | bytes 528
  824.4 35.9 %reduce-scatter.35.cloned.1.call-done = bf16[128,4]{1,0:T(8,128)(2,1)} async-done(((bf16[1024,4]{1,0:T(8,128)(2,1)}), bf16[128,4]{1,0:T(8,128)(2,1)}) %reduce-scatter.35.cloned.1.call-update) | async-done | bytes 1040
  861.6 35.7 %reduce-scatter.25.cloned.1.call-done = bf16[128,256]{1,0:T(8,128)(2,1)} async-done(((bf16[1024,256]{1,0:T(8,128)(2,1)}), bf16[128,256]{1,0:T(8,128)(2,1)}) %reduce-scatter.25.cloned.1.call-update) | async-done | bytes 65552 | tf_op jit(solution)/shard_map/reduce_scatter | solution.py:241
  899.2 14.3 %all-reduce = (f32[512]{0:T(512)}, f32[1024]{0:T(1024)}) all-reduce(f32[512]{0:T(512)S(1)} %add.409, f32[1024]{0:T(1024)S(1)} %add.412), channel_id=1, replica_groups=mesh['fsdp'=4,'ctx'=2,'tp'=4] {'fsdp','ctx'}, use_global_device_ids=true, to_apply=%region_37.38 | all-reduce | flops 1536 | bytes 12288 | tf_op jit(solution)/shard_map/psum | solution.py:257
  913.5 13.4 %reduce-scatter.23.cloned.1.call-done = bf16[2,64,1024]{2,1,0:T(8,128)(2,1)} async-done(((bf16[2,256,1024]{2,1,0:T(8,128)(2,1)}), bf16[2,64,1024]{2,1,0:T(8,128)(2,1)}) %reduce-scatter.23.cloned.1.call-update) | async-done | bytes 262160 | tf_op jit(solution)/shard_map/reduce_scatter | solution.py:223
  928.1 26.8 %reduce-scatter.19.cloned.1.call-done = bf16[2,64,1024]{2,1,0:T(8,128)(2,1)} async-done(((bf16[2,256,1024]{2,1,0:T(8,128)(2,1)}), bf16[2,64,1024]{2,1,0:T(8,128)(2,1)}) %reduce-scatter.19.cloned.1.call-update) | async-done | bytes 262160 | tf_op jit(solution)/shard_map/reduce_scatter | solution.py:223
  957.1 37.7 %reduce-scatter.31.cloned.1.call-done = bf16[128,768]{1,0:T(8,128)(2,1)} async-done(((bf16[1024,768]{1,0:T(8,128)(2,1)}), bf16[128,768]{1,0:T(8,128)(2,1)}) %reduce-scatter.31.cloned.1.call-update) | async-done | bytes 196624
  (304 shorter events, 159.0 us)
Async XLA Ops:
  8.0 75.6 %all-gather.5.cloned.1.call-start = ((), (), s32[]{:S(2)}) async-start(), calls=%async_computation.10 | async-start | bytes 1572864 | tf_op jit(solution)/shard_map/all_gather | solution.py:134
  8.1 8.6 collective-permute-start
  11.1 9.8 collective-permute-start.1
  13.3 29.1 %copy-start.20 = (bf16[1,2,256,1024]{3,2,1,0:T(8,128)(2,1)}, bf16[1,2,256,1024]{3,2,1,0:T(8,128)(2,1)S(1)}, u32[]{:S(2)}) copy-start(bf16[1,2,256,1024]{3,2,1,0:T(8,128)(2,1)S(1)} %get-tuple-element.113) | copy-start | bytes 3145732
  13.3 36.3 %copy-start.18 = (bf16[1,2,256,1024]{3,2,1,0:T(8,128)(2,1)}, bf16[1,2,256,1024]{3,2,1,0:T(8,128)(2,1)S(1)}, u32[]{:S(2)}) copy-start(bf16[1,2,256,1024]{3,2,1,0:T(8,128)(2,1)S(1)} %get-tuple-element.112) | copy-start | bytes 3145732
  16.7 8.3 collective-permute-start.2
  20.9 8.3 collective-permute-start.3
  25.0 8.4 collective-permute-start.4
  29.2 8.4 collective-permute-start.5
  33.4 8.3 collective-permute-start.6
  55.8 51.2 %copy-start.23 = (f32[2,256,4,1,64]{1,0,4,3,2:T(2,128)}, f32[2,256,4,1,64]{1,0,4,3,2:T(2,128)S(1)}, u32[]{:S(2)}) copy-start(f32[2,256,4,1,64]{1,0,4,3,2:T(2,128)S(1)} %get-tuple-element.114) | copy-start | bytes 1572868
  58.2 48.8 %all-gather.11.cloned.1.call-start = ((), (), s32[]{:S(2)}) async-start(), calls=%async_computation.13 | async-start | bytes 1572864 | tf_op jit(solution)/shard_map/all_gather | solution.py:134
  58.3 21.4 %copy-start.39 = (bf16[2,256,4,64]{1,3,2,0:T(8,128)(2,1)S(1)}, bf16[2,256,4,64]{1,3,2,0:T(8,128)(2,1)}, u32[]{:S(2)}) copy-start(bf16[2,256,4,64]{1,3,2,0:T(8,128)(2,1)} %get-tuple-element.144) | copy-start | bytes 786436
  80.5 191.4 %all-reduce.12.cloned.1.call-start = ((), (), s32[]{:S(2)}) async-start(), calls=%async_computation.26 | async-start | bytes 8388608 | tf_op jit(solution)/shard_map/psum | solution.py:74
  89.6 23.4 %copy-start.31 = (bf16[32,8,2,256]{3,1,2,0:T(8,128)(2,1)}, bf16[32,8,2,256]{3,1,2,0:T(8,128)(2,1)S(1)}, u32[]{:S(2)}) copy-start(bf16[32,8,2,256]{3,1,2,0:T(8,128)(2,1)S(1)} %copy.134) | copy-start | bytes 786436
  116.7 13.6 %copy-start.46 = (bf16[128,2]{0,1:T(2,128)(2,1)S(1)}, bf16[128,2]{0,1:T(2,128)(2,1)}, u32[]{:S(2)}) copy-start(bf16[128,2]{0,1:T(2,128)(2,1)} %param.20) | copy-start | bytes 1540
  116.7 160.0 %all-gather.7.cloned.1.call-start = ((), (), s32[]{:S(2)}) async-start(), calls=%async_computation.11 | async-start | bytes 2359296 | tf_op jit(solution)/shard_map/all_gather | solution.py:118
  117.3 176.3 %all-gather.9.cloned.1.call-start = ((), (), s32[]{:S(2)}) async-start(), calls=%async_computation.12 | async-start | bytes 2359296 | tf_op jit(solution)/shard_map/all_gather | solution.py:119
  117.9 337.1 %all-reduce.10.cloned.1.call-start = ((), (), s32[]{:S(2)}) async-start(), calls=%async_computation.25 | async-start | bytes 8388608 | tf_op jit(solution)/shard_map/psum | solution.py:74
  300.8 330.8 %all-reduce.8.cloned.1.call-start = ((), (), s32[]{:S(2)}) async-start(), calls=%async_computation.24 | async-start | bytes 8388608 | tf_op jit(solution)/shard_map/psum | solution.py:74
  477.5 214.4 %reduce-scatter.21.cloned.1.call-start = ((), (), s32[]{:S(2)}) async-start(), calls=%async_computation.16 | async-start | bytes 1572864 | tf_op jit(solution)/shard_map/reduce_scatter | solution.py:205
  655.3 45.0 %reduce-scatter.17.cloned.1.call-start = ((), (), s32[]{:S(2)}) async-start(), calls=%async_computation.14 | async-start | bytes 1572864 | tf_op jit(solution)/shard_map/reduce_scatter | solution.py:205
  667.3 74.7 %reduce-scatter.27.cloned.1.call-start = ((), (), s32[]{:S(2)}) async-start(), calls=%async_computation.19 | async-start | bytes 2359296 | tf_op jit(solution)/shard_map/reduce_scatter | solution.py:244
  673.9 112.4 %reduce-scatter.29.cloned.1.call-start = ((), (), s32[]{:S(2)}) async-start(), calls=%async_computation.20 | async-start | bytes 2359296 | tf_op jit(solution)/shard_map/reduce_scatter | solution.py:247
  680.3 142.6 %reduce-scatter.33.cloned.1.call-start = ((), (), s32[]{:S(2)}) async-start(), calls=%async_computation.22 | async-start | bytes 294912
  685.2 175.0 %reduce-scatter.35.cloned.1.call-start = ((), (), s32[]{:S(2)}) async-start(), calls=%async_computation.23 | async-start | bytes 294912
  686.3 211.1 %reduce-scatter.25.cloned.1.call-start = ((), (), s32[]{:S(2)}) async-start(), calls=%async_computation.18 | async-start | bytes 589824 | tf_op jit(solution)/shard_map/reduce_scatter | solution.py:241
  689.2 237.7 %reduce-scatter.23.cloned.1.call-start = ((), (), s32[]{:S(2)}) async-start(), calls=%async_computation.17 | async-start | bytes 1310720 | tf_op jit(solution)/shard_map/reduce_scatter | solution.py:223
  697.6 257.3 %reduce-scatter.19.cloned.1.call-start = ((), (), s32[]{:S(2)}) async-start(), calls=%async_computation.15 | async-start | bytes 1310720 | tf_op jit(solution)/shard_map/reduce_scatter | solution.py:223
  706.9 288.0 %reduce-scatter.31.cloned.1.call-start = ((), (), s32[]{:S(2)}) async-start(), calls=%async_computation.21 | async-start | bytes 1769472
  718.8 180.0 %copy-start.28 = (f32[2,256,4,128]{1,3,2,0:T(8,128)S(1)}, f32[2,256,4,128]{1,3,2,0:T(8,128)}, u32[]{:S(2)}) copy-start(f32[2,256,4,128]{1,3,2,0:T(8,128)} %copy-done.27) | copy-start | bytes 3145732
  718.8 180.1 %copy-start.26 = (f32[2,256,4,128]{1,3,2,0:T(8,128)S(1)}, f32[2,256,4,128]{1,3,2,0:T(8,128)}, u32[]{:S(2)}) copy-start(f32[2,256,4,128]{1,3,2,0:T(8,128)} %copy-done.25) | copy-start | bytes 3145732
  (51 other events, 152.8 us)
Sparse Core Ops, SparseCore 0:
  58.3 25.2 all-gather.4
  85.8 21.2 all-gather.10
  116.8 155.0 all-reduce.11
  301.0 153.9 all-reduce.9
  477.7 153.9 all-reduce.7
  655.4 19.3 reduce-scatter.20
  677.1 20.3 reduce-scatter.16
  700.8 41.1 reduce-scatter.26
  745.2 41.1 reduce-scatter.28
  789.2 33.6 reduce-scatter.32
  826.5 33.6 reduce-scatter.34
  863.1 34.1 reduce-scatter.24
  899.6 27.2 reduce-scatter.22
  929.1 25.7 reduce-scatter.18
  958.0 36.7 reduce-scatter.30
Sparse Core Ops, SparseCore 1:
  119.1 27.6 all-gather.6
  148.5 27.6 all-gather.8
